TPU v7x, 256 devices: a whole 4x4x8 slice. The times are simulated.
256 devices in a mesh: seq: 32 (over x, y, core), mp: 8 (over z).
Axes of the slice: x: 4, y: 4, z: 8, core: 2. Of those that a mesh axis runs over, the one named last changes fastest.
Arguments:
- hidden: bfloat16 [16, 4, 3584], P(None, None, 'seq'), may hold values from -40 to 40
- token_index_list: int32 [16, 4], replicated, may hold values from 0 to 31999
- embedding: bfloat16 [32000, 3584], P('mp', 'seq'), may hold values from -6 to 6
- attention_gain: bfloat16 [2, 3584], P(None, 'seq'), may hold values from 0.25 to 1.75
- query_key_value_matrix: bfloat16 [2, 3584, 3, 7168], P(None, 'seq', None, 'mp'), may hold values from -0.0625 to 0.0625
- attention_adapter_down: bfloat16 [2, 3584, 128], P(None, 'seq'), may hold values from -0.0625 to 0.0625
- attention_adapter_up: bfloat16 [128, 3, 7168], P(None, None, 'mp'), may hold values from -0.5 to 0.5
- cached_key_rows: bfloat16 [16, 4096, 7168], P(None, 'seq', 'mp'), may hold values from -240 to 240
- cached_value_rows: bfloat16 [16, 4096, 7168], P(None, 'seq', 'mp'), may hold values from -6 to 6
- lengths: int32 [16], replicated, may hold values from 1 to 4096, as said below
- output_matrix: bfloat16 [7168, 3584], P('mp', 'seq'), may hold values from -0.375 to 0.375
- feedforward_gain: bfloat16 [3584], P('seq'), may hold values from 0.25 to 1.75
- gate_matrix: bfloat16 [3584, 14336], P('seq', 'mp'), may hold values from -0.09375 to 0.09375
- up_matrix: bfloat16 [3584, 14336], P('seq', 'mp'), may hold values from -0.09375 to 0.09375
- feedforward_adapter_down: bfloat16 [3584, 128], P('seq'), may hold values from -0.09375 to 0.09375
- feedforward_adapter_up: bfloat16 [128, 2, 14336], P(None, None, 'mp'), may hold values from -0.5 to 0.5
- down_matrix: bfloat16 [14336, 3584], P('mp', 'seq'), may hold values from -0.046875 to 0.046875
Outputs:
- updated: bfloat16 [16, 4, 3584], P(None, None, 'seq')
- new_keys: bfloat16 [16, 4, 7168], P(None, None, 'mp')
- new_values: bfloat16 [16, 4, 7168], P(None, None, 'mp')
Inputs may be any that keep to these rules, and one draw needn't show every extreme that they name: `lengths`: heavy tailed, even in the logarithm; one request's cache is full, of 4096 positions.
All inputs are finite; a program needn't handle non-finite values.
Results may differ from a plain program's by a relative error of at most 0.02.
The roundings to bfloat16 on the way count: a program that leaves them out, or rounds other values in their place, can miss the bound.
Values may be sent and summed in bfloat16 or wider, within the bound.
A program may use at most 128 MiB of HBM per device.

v0:
```python
import jax
import jax.numpy as jnp
from jax import lax
from jax.sharding import PartitionSpec as P

MODEL_WIDTH = 3584
HEAD_DIM = 224


epsilon = 1e-05
masked_score = -1e30


def per_device(
    hidden,
    token_index_list,
    embedding,
    attention_gain,
    query_key_value_matrix,
    attention_adapter_down,
    attention_adapter_up,
    cached_key_rows,
    cached_value_rows,
    lengths,
    output_matrix,
    feedforward_gain,
    gate_matrix,
    up_matrix,
    feedforward_adapter_down,
    feedforward_adapter_up,
    down_matrix,
):
    requests, token_steps, local_width = hidden.shape
    row_count = requests * token_steps
    vocab_rows = embedding.shape[0]
    first_row = lax.axis_index("mp") * vocab_rows
    flat_ids = token_index_list.reshape(row_count)
    selector = (
        flat_ids[:, None] == first_row + jnp.arange(vocab_rows, dtype=jnp.int32)[None, :]
    ).astype(jnp.bfloat16)
    looked = jnp.dot(selector, embedding, preferred_element_type=jnp.float32)
    embedded = lax.psum(looked.astype(jnp.bfloat16), "mp")
    state_f = hidden.reshape(row_count, local_width).astype(jnp.float32)
    embed_f = embedded.astype(jnp.float32)
    gains = attention_gain.astype(jnp.float32)
    scaled_hidden = (state_f * gains[0]).astype(jnp.bfloat16)
    scaled_embedding = (embed_f * gains[1]).astype(jnp.bfloat16)
    head_total_width = query_key_value_matrix.shape[3]
    adapter_rank_size = attention_adapter_up.shape[0]
    wide_h = query_key_value_matrix[0].reshape(local_width, 3 * head_total_width)
    wide_e = query_key_value_matrix[1].reshape(local_width, 3 * head_total_width)
    proj_part = jnp.dot(scaled_hidden, wide_h, preferred_element_type=jnp.float32) + jnp.dot(
        scaled_embedding, wide_e, preferred_element_type=jnp.float32
    )
    adapter_piece = jnp.dot(
        scaled_hidden, attention_adapter_down[0], preferred_element_type=jnp.float32
    ) + jnp.dot(scaled_embedding, attention_adapter_down[1], preferred_element_type=jnp.float32)
    square_part = jnp.sum(state_f * state_f, 1) + jnp.sum(embed_f * embed_f, 1)
    up_rows_table = attention_adapter_up.reshape(adapter_rank_size, 3 * head_total_width)
    projection_total, adapter_total, square_sum = lax.psum(
        (proj_part, adapter_piece, square_part), "seq"
    )
    attention_scale = 1.0 / jnp.sqrt(square_sum / (2 * MODEL_WIDTH) + epsilon)
    attention_adapter_state = (adapter_total * attention_scale[:, None]).astype(jnp.bfloat16)
    projected_rows = (
        projection_total * attention_scale[:, None]
        + jnp.dot(attention_adapter_state, up_rows_table, preferred_element_type=jnp.float32)
    ).astype(jnp.bfloat16)
    projected_rows = projected_rows.reshape(requests, token_steps, 3, head_total_width)
    fresh_keys = projected_rows[:, :, 1]
    fresh_values = projected_rows[:, :, 2]
    head_count = head_total_width // HEAD_DIM
    positions = cached_key_rows.shape[1]
    inv_scale = 1.0 / jnp.sqrt(jnp.float32(HEAD_DIM))
    query_heads = projected_rows[:, :, 0].reshape(requests, token_steps, head_count, HEAD_DIM)
    cache_heads = cached_key_rows.reshape(requests, positions, head_count, HEAD_DIM)
    value_heads = cached_value_rows.reshape(requests, positions, head_count, HEAD_DIM)
    scores = (
        jnp.einsum("bthd,bphd->bhtp", query_heads, cache_heads, preferred_element_type=jnp.float32)
        * inv_scale
    )
    offset = lax.axis_index("seq") * positions
    live_mask = (offset + jnp.arange(positions, dtype=jnp.int32))[None, :] < lengths[:, None]
    live_wide = live_mask[:, None, None, :]
    scores = jnp.where(live_wide, scores, masked_score)
    local_peak = jnp.max(scores, -1)
    weights = jnp.where(live_wide, jnp.exp(scores - local_peak[..., None]), 0.0)
    local_total = jnp.sum(weights, -1)
    local_numer = jnp.einsum(
        "bhtp,bphd->bhtd",
        weights.astype(jnp.bfloat16),
        value_heads,
        preferred_element_type=jnp.float32,
    )
    merged_peak = lax.pmax(local_peak, "seq")
    factor = jnp.exp(local_peak - merged_peak)
    merged_total, merged_numer = lax.psum(
        (local_total * factor, local_numer * factor[..., None]), "seq"
    )
    fresh_key_heads = fresh_keys.reshape(requests, token_steps, head_count, HEAD_DIM)
    fresh_value_heads = fresh_values.reshape(requests, token_steps, head_count, HEAD_DIM)
    causal = jnp.arange(token_steps)[:, None] >= jnp.arange(token_steps)[None, :]
    new_scores = (
        jnp.einsum(
            "bthd,bjhd->bhtj", query_heads, fresh_key_heads, preferred_element_type=jnp.float32
        )
        * inv_scale
    )
    new_scores = jnp.where(causal, new_scores, masked_score)
    overall = jnp.maximum(merged_peak, jnp.max(new_scores, -1))
    new_weights = jnp.where(causal, jnp.exp(new_scores - overall[..., None]), 0.0)
    cache_factor = jnp.exp(merged_peak - overall)
    total_all = merged_total * cache_factor + jnp.sum(new_weights, -1)
    numer_all = merged_numer * cache_factor[..., None] + jnp.einsum(
        "bhtj,bjhd->bhtd",
        new_weights.astype(jnp.bfloat16),
        fresh_value_heads,
        preferred_element_type=jnp.float32,
    )
    attended = numer_all / total_all[..., None]
    attended = (
        jnp.transpose(attended, (0, 2, 1, 3))
        .reshape(row_count, head_total_width)
        .astype(jnp.bfloat16)
    )
    head_part = jnp.dot(attended, output_matrix, preferred_element_type=jnp.float32)
    mixed = lax.psum(head_part, "mp")
    mid = state_f + mixed
    square_mid = jnp.sum(mid * mid, 1)
    scaled_feedforward = (mid * feedforward_gain.astype(jnp.float32)).astype(jnp.bfloat16)
    adapter_piece2 = jnp.dot(
        scaled_feedforward, feedforward_adapter_down, preferred_element_type=jnp.float32
    )
    gate_part = jnp.dot(scaled_feedforward, gate_matrix, preferred_element_type=jnp.float32)
    up_partial = jnp.dot(scaled_feedforward, up_matrix, preferred_element_type=jnp.float32)
    gate_sum, up_sum, low_sum2, square_sum2 = lax.psum(
        (gate_part, up_partial, adapter_piece2, square_mid), "seq"
    )
    feedforward_scale = 1.0 / jnp.sqrt(square_sum2 / MODEL_WIDTH + epsilon)
    feedforward_adapter_state = (low_sum2 * feedforward_scale[:, None]).astype(jnp.bfloat16)
    gate_values = gate_sum * feedforward_scale[:, None] + jnp.dot(
        feedforward_adapter_state, feedforward_adapter_up[:, 0], preferred_element_type=jnp.float32
    )
    up_full = up_sum * feedforward_scale[:, None] + jnp.dot(
        feedforward_adapter_state, feedforward_adapter_up[:, 1], preferred_element_type=jnp.float32
    )
    activated = (jax.nn.gelu(gate_values, approximate=True) * up_full).astype(jnp.bfloat16)
    unit_part = jnp.dot(activated, down_matrix, preferred_element_type=jnp.float32)
    unit_total = lax.psum(unit_part, "mp")
    updated = (mid + unit_total).astype(jnp.bfloat16).reshape(requests, token_steps, local_width)
    return (updated, fresh_keys, fresh_values)


def solution(mesh):
    placed = (
        P(None, None, "seq"),
        P(),
        P("mp", "seq"),
        P(None, "seq"),
        P(None, "seq", None, "mp"),
        P(None, "seq", None),
        P(None, None, "mp"),
        P(None, "seq", "mp"),
        P(None, "seq", "mp"),
        P(),
        P("mp", "seq"),
        P("seq"),
        P("seq", "mp"),
        P("seq", "mp"),
        P("seq", None),
        P(None, None, "mp"),
        P("mp", "seq"),
    )
    return jax.shard_map(
        per_device,
        mesh=mesh,
        in_specs=placed,
        out_specs=(P(None, None, "seq"), P(None, None, "mp"), P(None, None, "mp")),
        check_vma=False,
    )
```

profile of v0, /device:TPU:32, one launch (start us, length us, event | category | flops | bytes accessed | tf_op | source)
XLA Modules:
  0.0 752.4 jit_solution(592174807731053906)
XLA Ops:
  8.9 29.4 %psum.84 = bf16[64,112]{1,0:T(8,128)(2,1)S(1)} all-reduce(bf16[64,112]{1,0:T(8,128)(2,1)S(1)} %convolution_convert_fusion), channel_id=1, replica_groups=mesh['seq'=32,'mp'=8] {'mp'}, use_global_device_ids=true, to_apply=%region_0.0 | all-reduce | flops 7168 | bytes 28672 | tf_op jit(solution)/shard_map/psum | solution.py:42
  39.0 2.2 fusion.46
  41.5 1.5 copy.115
  43.5 1.3 convolution_add_fusion.1
  45.3 124.2 %all-reduce.1 = (f32[64]{0:T(128)S(1)}, f32[64,128]{1,0:T(8,128)S(1)}) all-reduce(f32[64]{0:T(128)S(1)} %add.95, f32[64,128]{1,0:T(8,128)S(1)} %convolution_add_fusion.5), channel_id=1, replica_groups=mesh['seq'=32,'mp'=8] {'seq'}, use_global_device_ids=true, to_apply=%region_4.0 | all-reduce | flops 8256 | bytes 66048 | tf_op jit(solution)/shard_map/psum | solution.py:60
  169.5 2.2 fusion.47
  171.7 1.4 copy.116
  173.2 6.1 copy.118
  179.3 6.1 copy.120
  185.5 1.5 fusion
  187.1 1.9 fusion.48
  189.1 3.2 fusion.49
  192.3 123.8 %pmax.7 = f32[16,4,4]{2,1,0:T(4,128)S(1)} all-reduce(f32[16,4,4]{2,1,0:T(4,128)S(1)} %get-tuple-element.46), channel_id=1, replica_groups=mesh['seq'=32,'mp'=8] {'seq'}, use_global_device_ids=true, to_apply=%region_7.8 | all-reduce | flops 256 | bytes 2048 | tf_op jit(solution)/shard_map/pmax | solution.py:95
  317.5 123.8 %psum.89 = f32[16,4,4]{2,1,0:T(4,128)S(1)} all-reduce(f32[16,4,4]{2,1,0:T(4,128)S(1)} %bitcast.76), channel_id=1, replica_groups=mesh['seq'=32,'mp'=8] {'seq'}, use_global_device_ids=true, to_apply=%region_11.12 | all-reduce | flops 256 | bytes 2048 | tf_op jit(solution)/shard_map/psum | solution.py:97
  441.3 4.8 convolution_multiply_fusion
  446.5 107.2 %all-reduce.9.cloned.1.call-done = f32[16,4,4,224]{3,2,1,0:T(4,128)} async-done(((f32[16,4,4,224]{3,2,1,0:T(4,128)}), f32[16,4,4,224]{3,2,1,0:T(4,128)}) %all-reduce.9.cloned.1.call-update) | async-done | bytes 229392 | tf_op jit(solution)/shard_map/psum | solution.py:97
  553.7 1.3 fusion.6
  556.3 28.3 %psum.90 = f32[64,112]{1,0:T(8,128)S(1)} all-reduce(f32[64,112]{1,0:T(8,128)S(1)} %fusion.51), channel_id=1, replica_groups=mesh['seq'=32,'mp'=8] {'mp'}, use_global_device_ids=true, to_apply=%region_13.14 | all-reduce | flops 7168 | bytes 57344 | tf_op jit(solution)/shard_map/psum | solution.py:127
  584.8 2.0 fusion.52
  586.7 2.0 fusion.54
  590.3 123.8 %all-reduce = (f32[64]{0:T(128)S(1)}, f32[64,128]{1,0:T(8,128)S(1)}) all-reduce(f32[64]{0:T(128)S(1)} %get-tuple-element.24, f32[64,128]{1,0:T(8,128)S(1)} %fusion.53), channel_id=1, replica_groups=mesh['seq'=32,'mp'=8] {'seq'}, use_global_device_ids=true, to_apply=%region_16.17 | all-reduce | flops 8256 | bytes 66048 | tf_op jit(solution)/shard_map/psum | solution.py:136
  714.1 1.4 fusion.17
  715.5 1.6 fusion.4
  717.1 28.2 %psum.95 = f32[64,112]{1,0:T(8,128)S(1)} all-reduce(f32[64,112]{1,0:T(8,128)S(1)} %fusion.4), channel_id=1, replica_groups=mesh['seq'=32,'mp'=8] {'mp'}, use_global_device_ids=true, to_apply=%region_19.20 | all-reduce | flops 7168 | bytes 57344 | tf_op jit(solution)/shard_map/psum | solution.py:149
  (69 shorter events, 9.5 us)
Async XLA Ops:
  7.2 1.2 copy-start
  7.2 35.8 %copy-start.3 = (bf16[16,4,112]{2,1,0:T(4,128)(2,1)S(1)}, bf16[16,4,112]{2,1,0:T(4,128)(2,1)}, u32[]{:S(2)}) copy-start(bf16[16,4,112]{2,1,0:T(4,128)(2,1)} %param.17) | copy-start | bytes 43012
  7.2 178.3 %all-reduce.7.cloned.1.call-start = ((), (), s32[]{:S(2)}) async-start(), calls=%async_computation | async-start | bytes 1376256 | tf_op jit(solution)/shard_map/psum | solution.py:60
  41.1 3.8 copy-start.4
  41.1 128.4 %copy-start.1 = (bf16[128,2,1792]{2,1,0:T(2,128)(2,1)S(1)}, bf16[128,2,1792]{2,1,0:T(2,128)(2,1)}, u32[]{:S(2)}) copy-start(bf16[128,2,1792]{2,1,0:T(2,128)(2,1)} %param.32) | copy-start | bytes 2752516
  44.8 508.9 %all-reduce.9.cloned.1.call-start = ((), (), s32[]{:S(2)}) async-start(), calls=%async_computation.1 | async-start | bytes 524288 | tf_op jit(solution)/shard_map/psum | solution.py:97
  179.3 6.1 copy-start.7
  179.3 6.1 copy-start.6
  446.1 268.1 %all-reduce.11.cloned.1.call-start = ((), (), s32[]{:S(2)}) async-start(), calls=%async_computation.2 | async-start | bytes 1835008 | tf_op jit(solution)/shard_map/psum | solution.py:136
  553.7 36.5 %copy-start.5 = (bf16[112,128]{1,0:T(8,128)(2,1)S(1)}, bf16[112,128]{1,0:T(8,128)(2,1)}, u32[]{:S(2)}) copy-start(bf16[112,128]{1,0:T(8,128)(2,1)} %param.31) | copy-start | bytes 86020
  553.7 160.4 %copy-start.2 = (bf16[128,1,1792]{2,1,0:T(2,128)(2,1)S(1)}, bf16[128,1,1792]{2,1,0:T(2,128)(2,1)}, u32[]{:S(2)}) copy-start(bf16[128,1,1792]{2,1,0:T(2,128)(2,1)} %get-tuple-element.33) | copy-start | bytes 1376260
Sparse Core Ops, SparseCore 0:
  44.9 113.9 all-reduce.6
  446.2 107.4 all-reduce.8
  588.9 112.7 all-reduce.10
where the time goes:
time: 753 us; the launch traced here: 752 us
  blocking collectives  581 us (77%)
  waiting for transfers between devices  107 us (14%)
  local copies, waits for them, and re-layouts  25.8 us (3%)
  matrix products  21.5 us (3%)
  between operations  14 us (2%)
    psum x1, blocking collectives, per_device(): lax.psum((proj_part, adapter_piece, square_part), 'seq')  124 us
    psum x1, blocking collectives, per_device(): lax.psum((gate_part, up_partial, adapter_piece2, square_mid), 'seq')  124 us
    pmax x1, blocking collectives, per_device(): merged_peak = lax.pmax(local_peak, 'seq')  124 us
    psum x1, blocking collectives, per_device(): lax.psum((local_total * factor, local_numer * factor[..., None]), 'seq')  124 us
    psum x1, waiting for transfers between devices, per_device(): lax.psum((local_total * factor, local_numer * factor[..., None]), 'seq')  107 us
    psum x1, blocking collectives, per_device(): embedded = lax.psum(looked.astype(jnp.bfloat16), 'mp')  29.4 us
    psum x1, blocking collectives, per_device(): mixed = lax.psum(head_part, 'mp')  28.3 us
    psum x1, blocking collectives, per_device(): unit_total = lax.psum(unit_part, 'mp')  28.2 us
  transfers between devices with their start and end apart: 3, of which 1 were waited for; matrix products, arithmetic and copies ran while one was open for 2% of the time, Pallas kernels for 0%

commit v1 on v0

v1 whole, which is shorter than its diff:
```python
import jax
import jax.numpy as jnp
from jax import lax
from jax.experimental import pallas as pl
from jax.experimental.pallas import tpu as pltpu
from jax.sharding import PartitionSpec as P

MODEL_WIDTH = 3584
HEAD_DIM = 224
EPS = 1e-05
DEAD = -1e30

NS = 32
NM = 8
ROWS = 64
F = 112
FP = 128
CW = 896
HEADS = 4
UW = 1792
POS = 128
VR = 4000
REQ = 16
TOK = 4
RT = 16
NI = ROWS // RT
NJ = 7
OWN = NI * NJ

BF = jnp.bfloat16
F32 = jnp.float32
MESH = pl.DeviceIdType.MESH

DIMS_NT = (((1,), (1,)), ((), ()))


def mm(a, b):
    return jnp.dot(a, b, preferred_element_type=F32)


def mm_nt(a, b):
    return lax.dot_general(a, b, DIMS_NT, preferred_element_type=F32)


def head_of(col):
    one = jnp.int32(1)
    zero = jnp.int32(0)
    return (
        jnp.where(col >= HEAD_DIM, one, zero)
        + jnp.where(col >= 2 * HEAD_DIM, one, zero)
        + jnp.where(col >= 3 * HEAD_DIM, one, zero)
    )


def kernel(
    ids_hbm,
    len_hbm,
    hid_hbm,
    emb_hbm,
    gain_hbm,
    wqkv_hbm,
    adown_hbm,
    aup_hbm,
    kc_hbm,
    vc_hbm,
    wout_hbm,
    fgain_hbm,
    gate_hbm,
    upm_hbm,
    fdown_hbm,
    fup_hbm,
    down_hbm,
    upd_out,
    key_out,
    val_out,
    ids_v,
    len_s,
    hid_v,
    emb_v,
    gain_v,
    wq_v,
    ad_v,
    aup_v,
    kc_v,
    vc_v,
    wo_v,
    fgain_v,
    gate_v,
    upm_v,
    fd_v,
    fup_v,
    fu_v,
    dn_v,
    h_v,
    es_v,
    s2_v,
    r2_v,
    g_v,
    qm_v,
    s4_v,
    r4_v,
    a_v,
    hp_v,
    hr_v,
    mid_v,
    s7_v,
    r7_v,
    a2_v,
    dp_v,
    dr_v,
    fin_v,
    upd_v,
    key_v,
    val_v,
    lsem,
    ssem,
    rsem,
):
    me_s = lax.axis_index("seq")
    me_m = lax.axis_index("mp")
    mine = me_s < OWN
    my_i = lax.div(me_s, NJ)
    my_j = lax.rem(me_s, NJ)
    my_i = jnp.where(mine, my_i, 0)
    my_j = jnp.where(mine, my_j, 0)
    my_rows = pl.ds(pl.multiple_of(my_i * RT, RT), RT)

    barrier = pltpu.get_barrier_semaphore()

    def loop(n, me, fn):
        def body(k, carry):
            fn(lax.rem(me + 1 + k, n))
            return carry

        lax.fori_loop(0, n - 1, body, 0)

    def greet(axis):
        def fn(p):
            pl.semaphore_signal(barrier, inc=1, device_id={axis: p}, device_id_type=MESH)

        return fn

    loop(NS, me_s, greet("seq"))
    loop(NM, me_m, greet("mp"))

    local = []

    def fetch(src, dst):
        copy = pltpu.make_async_copy(src, dst, lsem.at[len(local)])
        copy.start()
        local.append(copy)
        return copy

    c_ids = fetch(ids_hbm, ids_v)
    c_emb = fetch(emb_hbm, emb_v)
    c_hid = fetch(hid_hbm, hid_v)
    c_gain = fetch(gain_hbm, gain_v)
    c_ad0 = fetch(adown_hbm.at[0], ad_v.at[pl.ds(0, F)])
    c_ad1 = fetch(adown_hbm.at[1], ad_v.at[pl.ds(FP, F)])
    c_wq0 = fetch(wqkv_hbm.at[0], wq_v.at[:, pl.ds(0, F)])
    c_wq1 = fetch(wqkv_hbm.at[1], wq_v.at[:, pl.ds(FP, F)])
    c_aup = fetch(aup_hbm, aup_v)
    c_len = fetch(len_hbm, len_s)
    c_kc = fetch(kc_hbm, kc_v)
    c_vc = fetch(vc_hbm, vc_v)
    c_wo = fetch(wout_hbm, wo_v.at[pl.ds(0, F)])
    c_fg = fetch(fgain_hbm, fgain_v)
    c_fup = fetch(fup_hbm, fup_v)
    c_fd = fetch(fdown_hbm, fd_v.at[pl.ds(0, F)])
    c_gate = fetch(gate_hbm, gate_v.at[pl.ds(0, F)])
    c_upm = fetch(upm_hbm, upm_v.at[pl.ds(0, F)])
    c_dn = fetch(down_hbm, dn_v.at[pl.ds(0, F)])

    pad = FP - F
    wq_v[:, pl.ds(F, pad), :] = jnp.zeros((3, pad, CW), BF)
    wq_v[:, pl.ds(FP + F, pad), :] = jnp.zeros((3, pad, CW), BF)
    ad_v[pl.ds(F, pad), :] = jnp.zeros((pad, FP), BF)
    ad_v[pl.ds(FP + F, pad), :] = jnp.zeros((pad, FP), BF)
    wo_v[pl.ds(F, pad), :] = jnp.zeros((pad, CW), BF)
    fd_v[pl.ds(F, pad), :] = jnp.zeros((pad, FP), BF)
    gate_v[pl.ds(F, pad), :] = jnp.zeros((pad, UW), BF)
    upm_v[pl.ds(F, pad), :] = jnp.zeros((pad, UW), BF)
    dn_v[pl.ds(F, pad), :] = jnp.zeros((pad, UW), BF)
    h_v[...] = jnp.zeros((ROWS, FP), F32)

    def took(ref, sem):
        pltpu.make_async_copy(ref, ref, sem).wait()

    def send(src, dst, phase, axis, p):
        pltpu.make_async_remote_copy(
            src_ref=src,
            dst_ref=dst,
            send_sem=ssem.at[phase],
            recv_sem=rsem.at[phase],
            device_id={axis: p},
            device_id_type=MESH,
        ).start()

    def scatter(src_of, dst, phase):
        def fn(p):
            @pl.when(p < OWN)
            def _():
                send(src_of(lax.div(p, NJ), lax.rem(p, NJ)), dst, phase, "seq", p)

        loop(NS, me_s, fn)

    def gather(ref, phase):
        loop(NS, me_s, lambda p: send(ref, ref, phase, "seq", p))

    c_ids.wait()
    ids = ids_v[...]
    high = ids // 256
    low = ids - high * 256
    spread = (
        lax.broadcasted_iota(jnp.int32, (REQ, ROWS), 0)
        == lax.broadcasted_iota(jnp.int32, (REQ, ROWS), 1) // TOK
    ).astype(F32).astype(BF)
    wide = mm(high.astype(F32).astype(BF), spread) * 256.0 + mm(low.astype(F32).astype(BF), spread)
    pick = lax.broadcasted_iota(jnp.int32, (TOK, ROWS), 0) == (
        lax.broadcasted_iota(jnp.int32, (TOK, ROWS), 1) % TOK
    )
    id_row = jnp.sum(jnp.where(pick, wide, 0.0), 0, keepdims=True).astype(jnp.int32)
    id_row = id_row - me_m * VR
    selector = (
        (lax.broadcasted_iota(jnp.int32, (VR, ROWS), 0) == id_row).astype(F32).astype(BF)
    )
    c_emb.wait()
    found = mm(emb_v[...], selector)
    found = jnp.concatenate([found, jnp.zeros((pad, ROWS), F32)], 0)
    es_v[me_m] = found.T.astype(BF)

    pl.semaphore_wait(barrier, NS + NM - 2)

    loop(NM, me_m, lambda p: send(es_v.at[me_m], es_v.at[me_m], 0, "mp", p))

    c_hid.wait()
    c_gain.wait()
    for b in range(REQ):
        h_v[pl.ds(TOK * b, TOK), pl.ds(0, F)] = hid_v[b].astype(F32)
    gains = gain_v[...].astype(F32)
    gains = jnp.concatenate([gains, jnp.zeros((2, pad), F32)], 1)
    state = h_v[...]
    scaled_h = (state * gains[0:1]).astype(BF)
    c_ad0.wait()
    c_ad1.wait()
    c_wq0.wait()
    c_wq1.wait()
    c_aup.wait()

    took(es_v.at[pl.ds(0, NM - 1)], rsem.at[0])
    embed = es_v[0].astype(F32)
    for q in range(1, NM):
        embed = embed + es_v[q].astype(F32)
    scaled_e = (embed * gains[1:2]).astype(BF)
    both = jnp.concatenate([scaled_h, scaled_e], 1)
    squares = jnp.sum(state * state + embed * embed, 1, keepdims=True)
    squares = jnp.broadcast_to(squares, (ROWS, 128)).astype(BF)
    low1 = mm(both, ad_v[...]).astype(BF)
    for part in range(3):
        proj = mm(both, wq_v[part]) + mm(low1, aup_v[part])
        for j in range(NJ):
            s2_v[j, :, pl.ds(128 * part, 128)] = proj[:, 128 * j : 128 * j + 128].astype(BF)
    for j in range(NJ):
        s2_v[j, :, pl.ds(384, 128)] = squares

    def block2(i, j):
        return s2_v.at[j, pl.ds(pl.multiple_of(i * RT, RT), RT)]

    scatter(block2, r2_v.at[me_s], 1)

    @pl.when(mine)
    def _():
        r2_v[me_s] = s2_v[my_j, my_rows, :]
        took(r2_v.at[pl.ds(0, NS - 1)], rsem.at[1])
        total = r2_v[0].astype(F32)
        for s in range(1, NS):
            total = total + r2_v[s].astype(F32)
        scale = 1.0 / jnp.sqrt(total[:, 384:] / (2 * MODEL_WIDTH) + EPS)
        for part in range(3):
            g_v[my_j, my_rows, pl.ds(128 * part, 128)] = (
                total[:, 128 * part : 128 * part + 128] * scale
            ).astype(BF)
        gather(g_v.at[my_j, my_rows], 2)
        took(r2_v.at[pl.ds(0, OWN - 1), :, pl.ds(0, 384)], rsem.at[2])

    @pl.when(jnp.logical_not(mine))
    def _():
        took(r2_v.at[pl.ds(0, OWN), :, pl.ds(0, 384)], rsem.at[2])

    lane = lax.broadcasted_iota(jnp.int32, (RT, 128), 1)
    for i in range(NI):
        rows = pl.ds(RT * i, RT)
        for c in range(NJ):
            q = g_v[c, rows, pl.ds(0, 128)].astype(F32)
            first, last = (128 * c) // HEAD_DIM, (128 * c + 127) // HEAD_DIM
            for h in range(HEADS):
                if first == last == h:
                    part = q
                elif h in (first, last):
                    part = jnp.where(head_of(lane + 128 * c) == h, q, 0.0)
                else:
                    part = jnp.zeros((RT, 128), F32)
                qm_v[i, pl.ds(RT * h, RT), pl.ds(128 * c, 128)] = part.astype(BF)

    inv_scale = 1.0 / (HEAD_DIM**0.5)
    c_len.wait()
    c_kc.wait()
    c_vc.wait()
    place = me_s * POS + lax.broadcasted_iota(jnp.int32, (HEADS * RT, POS), 1)
    group = (lax.broadcasted_iota(jnp.int32, (HEADS * RT, POS), 0) % RT) // TOK
    for i in range(NI):
        score = jnp.full((HEADS * RT, POS), DEAD, F32)
        for k in range(RT // TOK):
            b = (RT // TOK) * i + k
            one = mm_nt(qm_v[i], kc_v[b]) * inv_scale
            score = jnp.where((group == k) & (place < len_s[b]), one, score)
        peak = jnp.max(score, 1, keepdims=True)
        weight = jnp.where(score > 0.5 * DEAD, jnp.exp(score - peak), 0.0)
        total = jnp.sum(weight, 1, keepdims=True)
        spread_w = jnp.concatenate(
            [jnp.where(group == k, weight, 0.0).astype(BF) for k in range(RT // TOK)], 1
        )
        values = vc_v[pl.ds((RT // TOK) * i, RT // TOK)].reshape((RT // TOK) * POS, CW)
        numer = mm(spread_w, values)
        live = total > 0.0
        safe = jnp.where(live, total, 1.0)
        lse = jnp.where(live, peak + jnp.log(safe), DEAD)
        inverse = 1.0 / safe
        stats = jnp.zeros((RT, 128), F32)
        for h in range(HEADS):
            rest = jnp.broadcast_to(lse[RT * h : RT * h + RT], (RT, 128))
            for piece in range(3):
                lead = rest.astype(BF).astype(F32)
                stats = jnp.where(lane == 3 * h + piece, lead, stats)
                rest = rest - lead
        stats = stats.astype(BF)
        rows = pl.ds(RT * i, RT)
        for c in range(NJ):
            first, last = (128 * c) // HEAD_DIM, (128 * c + 127) // HEAD_DIM
            cols = slice(128 * c, 128 * c + 128)
            here = numer[RT * first : RT * first + RT, cols] * inverse[RT * first : RT * first + RT]
            if last != first:
                there = numer[RT * last : RT * last + RT, cols] * inverse[RT * last : RT * last + RT]
                here = jnp.where(head_of(lane + 128 * c) == first, here, there)
            s4_v[c, rows, pl.ds(0, 128)] = here.astype(BF)
            s4_v[c, rows, pl.ds(128, 128)] = stats

    def block4(i, j):
        return s4_v.at[j, pl.ds(pl.multiple_of(i * RT, RT), RT)]

    scatter(block4, r4_v.at[me_s], 3)

    @pl.when(mine)
    def _():
        r4_v[me_s] = s4_v[my_j, my_rows, :]
        lane_head = head_of(lane + 128 * my_j)
        head_a = head_of(128 * my_j)
        head_b = head_of(128 * my_j + 127)
        q = jnp.concatenate([g_v[c, my_rows, pl.ds(0, 128)] for c in range(NJ)], 1).astype(F32)
        k = jnp.concatenate([g_v[c, my_rows, pl.ds(128, 128)] for c in range(NJ)], 1)
        v = g_v[my_j, my_rows, pl.ds(256, 128)]
        col_head = head_of(lax.broadcasted_iota(jnp.int32, (RT, CW), 1))
        r_at = lax.broadcasted_iota(jnp.int32, (RT, RT), 0)
        c_at = lax.broadcasted_iota(jnp.int32, (RT, RT), 1)
        seen = (r_at // TOK == c_at // TOK) & (c_at % TOK <= r_at % TOK)

        def fresh(head):
            score = mm_nt(jnp.where(col_head == head, q, 0.0).astype(BF), k) * inv_scale
            score = jnp.where(seen, score, DEAD)
            peak = jnp.max(score, 1, keepdims=True)
            weight = jnp.where(seen, jnp.exp(score - peak), 0.0)
            total = jnp.sum(weight, 1, keepdims=True)
            return mm(weight.astype(BF), v) / total, peak + jnp.log(total)

        out_a, lse_a = fresh(head_a)
        out_b, lse_b = fresh(head_b)
        new_out = jnp.where(lane_head == head_a, out_a, out_b)
        new_lse = jnp.where(lane_head == head_a, lse_a, lse_b)

        stat_head = lax.broadcasted_iota(jnp.int32, (128, 128), 0) // 3
        expand = (
            (stat_head == head_of(lax.broadcasted_iota(jnp.int32, (128, 128), 1) + 128 * my_j))
            .astype(F32)
            .astype(BF)
        )
        took(r4_v.at[pl.ds(0, NS - 1)], rsem.at[3])
        stats = r4_v[:, :, pl.ds(128, 128)].reshape(NS * RT, 128)
        lse = mm(stats, expand).reshape(NS, RT, 128)
        peak = jnp.maximum(jnp.max(lse, 0), new_lse)
        weight = jnp.exp(lse - peak[None])
        new_weight = jnp.exp(new_lse - peak)
        total = jnp.sum(weight, 0) + new_weight
        numer = jnp.sum(weight * r4_v[:, :, pl.ds(0, 128)].astype(F32), 0) + new_weight * new_out
        block = a_v.at[my_rows, pl.ds(pl.multiple_of(my_j * 128, 128), 128)]
        block[...] = (numer / total).astype(BF)
        gather(block, 4)

    for b in range(REQ):
        for c in range(NJ):
            key_v[b, :, pl.ds(128 * c, 128)] = g_v[c, pl.ds(TOK * b, TOK), pl.ds(128, 128)]
            val_v[b, :, pl.ds(128 * c, 128)] = g_v[c, pl.ds(TOK * b, TOK), pl.ds(256, 128)]
    o_key = pltpu.make_async_copy(key_v, key_out, lsem.at[len(local)])
    o_val = pltpu.make_async_copy(val_v, val_out, lsem.at[len(local) + 1])
    o_key.start()
    o_val.start()
    c_fup.wait()

    def split(k, carry):
        at = pl.ds(pl.multiple_of(k * 16, 16), 16)
        two = fup_v[at].astype(F32)
        fu_v[0, at, :] = two[:, 0, :].astype(BF)
        fu_v[1, at, :] = two[:, 1, :].astype(BF)
        return carry

    lax.fori_loop(0, 8, split, 0)
    c_wo.wait()

    @pl.when(mine)
    def _():
        took(r4_v.at[pl.ds(0, OWN - 1), :, pl.ds(0, 128)], rsem.at[4])

    @pl.when(jnp.logical_not(mine))
    def _():
        took(r4_v.at[pl.ds(0, OWN), :, pl.ds(0, 128)], rsem.at[4])

    my_eight = pl.ds(pl.multiple_of(me_m * 8, 8), 8)

    def sum_mp(part_v, slot_v, phase):
        def fn(p):
            send(
                part_v.at[pl.ds(pl.multiple_of(p * 8, 8), 8)], slot_v.at[me_m], phase, "mp", p
            )

        loop(NM, me_m, fn)
        slot_v[me_m] = part_v[my_eight, :]
        took(slot_v.at[pl.ds(0, NM - 1)], rsem.at[phase])
        total = slot_v[0]
        for q in range(1, NM):
            total = total + slot_v[q]
        return total

    hp_v[...] = mm_nt(a_v[...], wo_v[...])
    mixed = sum_mp(hp_v, hr_v, 5)
    mid_v[my_eight, :] = mixed + h_v[my_eight, :]
    loop(NM, me_m, lambda p: send(mid_v.at[my_eight], mid_v.at[my_eight], 6, "mp", p))
    c_fg.wait()
    c_fd.wait()
    c_gate.wait()
    c_upm.wait()
    fgain = jnp.concatenate([fgain_v[...].astype(F32), jnp.zeros((1, pad), F32)], 1)
    took(hr_v.at[pl.ds(0, NM - 1)], rsem.at[6])

    mid = mid_v[...]
    scaled_m = (mid * fgain).astype(BF)
    squares = jnp.broadcast_to(jnp.sum(mid * mid, 1, keepdims=True), (ROWS, 128)).astype(BF)
    low2 = mm(scaled_m, fd_v[...]).astype(BF)
    for part, w_v in enumerate((gate_v, upm_v)):
        proj = mm(scaled_m, w_v[...]) + mm(low2, fu_v[part])
        for j in range(NJ):
            s7_v[j, :, pl.ds(256 * part, 256)] = proj[:, 256 * j : 256 * j + 256].astype(BF)
    for j in range(NJ):
        s7_v[j, :, pl.ds(512, 128)] = squares

    def block7(i, j):
        return s7_v.at[j, pl.ds(pl.multiple_of(i * RT, RT), RT)]

    scatter(block7, r7_v.at[me_s], 7)

    @pl.when(mine)
    def _():
        r7_v[me_s] = s7_v[my_j, my_rows, :]
        took(r7_v.at[pl.ds(0, NS - 1)], rsem.at[7])
        total = r7_v[0].astype(F32)
        for s in range(1, NS):
            total = total + r7_v[s].astype(F32)
        scale = 1.0 / jnp.sqrt(total[:, 512:] / MODEL_WIDTH + EPS)
        scale = jnp.concatenate([scale, scale], 1)
        gate = total[:, 0:256] * scale
        up = total[:, 256:512] * scale
        block = a2_v.at[my_rows, pl.ds(pl.multiple_of(my_j * 256, 256), 256)]
        block[...] = (jax.nn.gelu(gate, approximate=True) * up).astype(BF)
        gather(block, 8)
        took(r4_v.at[pl.ds(0, OWN - 1)], rsem.at[8])

    @pl.when(jnp.logical_not(mine))
    def _():
        took(r4_v.at[pl.ds(0, OWN)], rsem.at[8])

    c_dn.wait()
    dp_v[...] = mm_nt(a2_v[...], dn_v[...])
    down = sum_mp(dp_v, dr_v, 9)
    fin_v[my_eight, :] = down + mid_v[my_eight, :]
    loop(NM, me_m, lambda p: send(fin_v.at[my_eight], fin_v.at[my_eight], 10, "mp", p))
    took(dr_v.at[pl.ds(0, NM - 1)], rsem.at[10])
    for b in range(REQ):
        upd_v[b] = fin_v[pl.ds(TOK * b, TOK), pl.ds(0, F)].astype(BF)
    o_upd = pltpu.make_async_copy(upd_v, upd_out, lsem.at[len(local) + 2])
    o_upd.start()

    took(es_v.at[pl.ds(0, NM - 1)], ssem.at[0])
    took(hr_v.at[pl.ds(0, NM - 1)], ssem.at[5])
    took(hr_v.at[pl.ds(0, NM - 1)], ssem.at[6])
    took(dr_v.at[pl.ds(0, NM - 1)], ssem.at[9])
    took(dr_v.at[pl.ds(0, NM - 1)], ssem.at[10])

    @pl.when(mine)
    def _():
        took(r2_v.at[pl.ds(0, OWN - 1)], ssem.at[1])
        took(r2_v.at[pl.ds(0, NS - 1), :, pl.ds(0, 384)], ssem.at[2])
        took(r4_v.at[pl.ds(0, OWN - 1)], ssem.at[3])
        took(r4_v.at[pl.ds(0, NS - 1), :, pl.ds(0, 128)], ssem.at[4])
        took(r7_v.at[pl.ds(0, OWN - 1)], ssem.at[7])
        took(r4_v.at[pl.ds(0, NS - 1)], ssem.at[8])

    @pl.when(jnp.logical_not(mine))
    def _():
        took(r2_v.at[pl.ds(0, OWN)], ssem.at[1])
        took(r4_v.at[pl.ds(0, OWN)], ssem.at[3])
        took(r7_v.at[pl.ds(0, OWN)], ssem.at[7])

    o_key.wait()
    o_val.wait()
    o_upd.wait()


def per_device(
    hidden,
    token_index_list,
    embedding,
    attention_gain,
    query_key_value_matrix,
    attention_adapter_down,
    attention_adapter_up,
    cached_key_rows,
    cached_value_rows,
    lengths,
    output_matrix,
    feedforward_gain,
    gate_matrix,
    up_matrix,
    feedforward_adapter_down,
    feedforward_adapter_up,
    down_matrix,
):
    hbm = pl.BlockSpec(memory_space=pl.ANY)
    vm = pltpu.VMEM
    return pl.pallas_call(
        kernel,
        name="block",
        out_shape=(
            jax.ShapeDtypeStruct((REQ, TOK, F), BF),
            jax.ShapeDtypeStruct((REQ, TOK, CW), BF),
            jax.ShapeDtypeStruct((REQ, TOK, CW), BF),
        ),
        in_specs=[hbm] * 17,
        out_specs=(hbm, hbm, hbm),
        scratch_shapes=[
            vm((TOK, REQ), jnp.int32),
            pltpu.SMEM((REQ,), jnp.int32),
            vm((REQ, TOK, F), BF),
            vm((F, VR), BF),
            vm((2, F), BF),
            vm((3, 2 * FP, CW), BF),
            vm((2 * FP, 128), BF),
            vm((3, 128, CW), BF),
            vm((REQ, POS, CW), BF),
            vm((REQ, POS, CW), BF),
            vm((FP, CW), BF),
            vm((1, F), BF),
            vm((FP, UW), BF),
            vm((FP, UW), BF),
            vm((FP, 128), BF),
            vm((128, 2, UW), BF),
            vm((2, 128, UW), BF),
            vm((FP, UW), BF),
            vm((ROWS, FP), F32),
            vm((NM, ROWS, FP), BF),
            vm((NJ, ROWS, 512), BF),
            vm((NS, RT, 512), BF),
            vm((NJ, ROWS, 384), BF),
            vm((NI, HEADS * RT, CW), BF),
            vm((NJ, ROWS, 256), BF),
            vm((NS, RT, 256), BF),
            vm((ROWS, CW), BF),
            vm((ROWS, FP), F32),
            vm((NM, 8, FP), F32),
            vm((ROWS, FP), F32),
            vm((NJ, ROWS, 640), BF),
            vm((NS, RT, 640), BF),
            vm((ROWS, UW), BF),
            vm((ROWS, FP), F32),
            vm((NM, 8, FP), F32),
            vm((ROWS, FP), F32),
            vm((REQ, TOK, F), BF),
            vm((REQ, TOK, CW), BF),
            vm((REQ, TOK, CW), BF),
            pltpu.SemaphoreType.DMA((24,)),
            pltpu.SemaphoreType.DMA((11,)),
            pltpu.SemaphoreType.DMA((11,)),
        ],
        compiler_params=pltpu.CompilerParams(
            collective_id=0, has_side_effects=True, vmem_limit_bytes=56 * 1024 * 1024
        ),
    )(
        token_index_list.T,
        lengths,
        hidden,
        embedding.T,
        attention_gain,
        jnp.transpose(query_key_value_matrix, (0, 2, 1, 3)),
        attention_adapter_down,
        jnp.transpose(attention_adapter_up, (1, 0, 2)),
        cached_key_rows,
        cached_value_rows,
        output_matrix.T,
        feedforward_gain.reshape(1, F),
        gate_matrix,
        up_matrix,
        feedforward_adapter_down,
        feedforward_adapter_up,
        down_matrix.T,
    )


def solution(mesh):
    placed = (
        P(None, None, "seq"),
        P(),
        P("mp", "seq"),
        P(None, "seq"),
        P(None, "seq", None, "mp"),
        P(None, "seq", None),
        P(None, None, "mp"),
        P(None, "seq", "mp"),
        P(None, "seq", "mp"),
        P(),
        P("mp", "seq"),
        P("seq"),
        P("seq", "mp"),
        P("seq", "mp"),
        P("seq", None),
        P(None, None, "mp"),
        P("mp", "seq"),
    )
    return jax.shard_map(
        per_device,
        mesh=mesh,
        in_specs=placed,
        out_specs=(P(None, None, "seq"), P(None, None, "mp"), P(None, None, "mp")),
        check_vma=False,
    )
```

time: 753 us -> 90.2 us (0.12)
  blocking collectives: 581 us -> 0 us
  waiting for transfers between devices: 107 us -> 0 us
  Pallas kernels: 0 us -> 83.9 us
  matrix products: 21.5 us -> 0 us
  local copies, waits for them, and re-layouts: 25.8 us -> 4.5 us
  between operations: 14 us -> 0.65 us
    psum x6 -> x0, blocking collectives: 458 us -> none  [the longest x1 124 us: per_device(): lax.psum((proj_part, adapter_piece, square_part), 'seq')]
    pmax x1 -> x0, blocking collectives: 124 us -> none  [per_device(): merged_peak = lax.pmax(local_peak, 'seq')]
    psum x3 -> x0, waiting for transfers between devices: 107 us -> none  [the longest x1 107 us: per_device(): lax.psum((local_total * factor, local_numer * factor[..., None]), 'seq')]
    pallas_call x0 -> x1, Pallas kernels: none -> 83.9 us  [per_device(): pl.pallas_call(kernel, name='block', out_shape=(jax.ShapeDtypeStruct((REQ...]
    dot_general x16 -> x0, matrix products: 21.5 us -> none  [the longest x1 4.76 us: per_device(): jnp.einsum('bhtp,bphd->bhtd', weights.astype(jnp.bfloat16), value_heads,...]
    unnamed x22 -> x3, local copies, waits for them, and re-layouts: 16.1 us -> 4.5 us
    slice x5 -> x0, local copies, waits for them, and re-layouts: 8.07 us -> none  [the longest x2 3.62 us: per_device(): query_key_value_matrix[1].reshape(local_width, 3 * head_total_width)]
  transfers between devices with their start and end apart: 3 -> 0, of which waited for: 1 -> 0; matrix products, arithmetic and copies ran while one was open for 2% -> 0% of each run, Pallas kernels for 0% -> 0%
where the time goes in v1:
time: 90.2 us; the launch traced here: 89 us
  Pallas kernels  83.9 us (93%)
  local copies, waits for them, and re-layouts  4.5 us (5%)
    pallas_call x1, Pallas kernels, per_device(): pl.pallas_call(kernel, name='block', out_shape=(jax.ShapeDtypeStruct((REQ...  83.9 us
    unnamed x3, local copies, waits for them, and re-layouts  4.5 us

profile of v1, /device:TPU:32, one launch (start us, length us, event | category | flops | bytes accessed | tf_op | source)
XLA Modules:
  0.0 89.0 jit_solution(17046263964405133507)
XLA Ops:
  0.6 83.9 %block.1 = (bf16[16,4,112]{2,1,0:T(4,128)(2,1)}, bf16[16,4,896]{2,1,0:T(4,128)(2,1)}, bf16[16,4,896]{2,1,0:T(4,128)(2,1)}) custom-call(s32[4,16]{1,0:T(4,128)} %bitcast.12, s32[16]{0:T(128)} %len_hbm.1, bf16[16,4,112]{2,1,0:T(4,128)(2,1)} %hid_hbm.1, bf16[112,4000]{1,0:T(8,128)(2,1)} %bitcast.8, bf16[2,112]{1,0:T(2,128)(2,1)} %gain_hbm.1, ...), custom_call_target="tpu_custom_call" | custom-call | tf_op jit(solution)/shard_map/block/pallas_call | solution.py:547
  84.6 1.3 %copy.23 = bf16[16,4,112]{2,1,0:T(4,128)(2,1)} copy(bf16[16,4,112]{2,1,0:T(4,128)(2,1)} %get-tuple-element.6) | data formatting | bytes 28672
  85.9 1.6 %copy.24 = bf16[16,4,896]{2,1,0:T(4,128)(2,1)} copy(bf16[16,4,896]{2,1,0:T(4,128)(2,1)} %get-tuple-element.7) | data formatting | bytes 229376
  87.5 1.6 %copy.25 = bf16[16,4,896]{2,1,0:T(4,128)(2,1)} copy(bf16[16,4,896]{2,1,0:T(4,128)(2,1)} %get-tuple-element.8) | data formatting | bytes 229376

commit v2 on v1

--- a/solution.py
+++ b/solution.py
@@ -26,6 +26,17 @@
 NI = ROWS // RT
 NJ = 7
 OWN = NI * NJ
+
+def hops(offset):
+    dx, dy, dc = offset
+    return min(dx, 4 - dx) + min(dy, 4 - dy)
+
+
+SEQ_ORDER = sorted(
+    ((dx, dy, dc) for dx in range(4) for dy in range(4) for dc in range(2) if dx or dy or dc),
+    key=lambda offset: -hops(offset),
+)
+MP_ORDER = (4, 3, 5, 2, 6, 1, 7)
 
 BF = jnp.bfloat16
 F32 = jnp.float32
@@ -70,9 +81,9 @@
     fdown_hbm,
     fup_hbm,
     down_hbm,
-    upd_out,
-    key_out,
-    val_out,
+    upd_v,
+    key_v,
+    val_v,
     ids_v,
     len_s,
     hid_v,
@@ -92,26 +103,26 @@
     fu_v,
     dn_v,
     h_v,
+    ph_v,
     es_v,
     s2_v,
     r2_v,
+    s2k_v,
+    r2k_v,
+    gq_v,
     g_v,
     qm_v,
     s4_v,
     r4_v,
     a_v,
-    hp_v,
     hr_v,
     mid_v,
+    x7_v,
+    p7_v,
     s7_v,
     r7_v,
     a2_v,
-    dp_v,
     dr_v,
-    fin_v,
-    upd_v,
-    key_v,
-    val_v,
     lsem,
     ssem,
     rsem,
@@ -127,12 +138,20 @@
 
     barrier = pltpu.get_barrier_semaphore()
 
-    def loop(n, me, fn):
-        def body(k, carry):
-            fn(lax.rem(me + 1 + k, n))
-            return carry
-
-        lax.fori_loop(0, n - 1, body, 0)
+    x = lax.div(me_s, 8)
+    y = lax.rem(lax.div(me_s, 2), 4)
+    core = lax.rem(me_s, 2)
+
+    def each_seq(fn):
+        for dx, dy, dc in SEQ_ORDER:
+            px = lax.rem(x + dx, 4) if dx else x
+            py = lax.rem(y + dy, 4) if dy else y
+            pc = 1 - core if dc else core
+            fn((px * 4 + py) * 2 + pc)
+
+    def each_mp(fn):
+        for d in MP_ORDER:
+            fn(lax.rem(me_m + d, NM))
 
     def greet(axis):
         def fn(p):
@@ -140,8 +159,8 @@
 
         return fn
 
-    loop(NS, me_s, greet("seq"))
-    loop(NM, me_m, greet("mp"))
+    each_mp(greet("mp"))
+    each_seq(greet("seq"))
 
     local = []
 
@@ -202,10 +221,10 @@
             def _():
                 send(src_of(lax.div(p, NJ), lax.rem(p, NJ)), dst, phase, "seq", p)
 
-        loop(NS, me_s, fn)
+        each_seq(fn)
 
     def gather(ref, phase):
-        loop(NS, me_s, lambda p: send(ref, ref, phase, "seq", p))
+        each_seq(lambda p: send(ref, ref, phase, "seq", p))
 
     c_ids.wait()
     ids = ids_v[...]
@@ -231,7 +250,7 @@
 
     pl.semaphore_wait(barrier, NS + NM - 2)
 
-    loop(NM, me_m, lambda p: send(es_v.at[me_m], es_v.at[me_m], 0, "mp", p))
+    each_mp(lambda p: send(es_v.at[me_m], es_v.at[me_m], 0, "mp", p))
 
     c_hid.wait()
     c_gain.wait()
@@ -243,55 +262,73 @@
     scaled_h = (state * gains[0:1]).astype(BF)
     c_ad0.wait()
     c_ad1.wait()
+    c_aup.wait()
     c_wq0.wait()
     c_wq1.wait()
-    c_aup.wait()
+    low_h = mm(scaled_h, ad_v[pl.ds(0, FP), :]).astype(BF)
+    low_w = ad_v[pl.ds(FP, FP), :]
+    for part in range(3):
+        ph_v[part] = mm(scaled_h, wq_v[part, pl.ds(0, FP), :]) + mm(low_h, aup_v[part])
+        wq_v[part, pl.ds(FP, FP), :] = (
+            wq_v[part, pl.ds(FP, FP), :].astype(F32) + mm(low_w, aup_v[part])
+        ).astype(BF)
+    squares_h = jnp.sum(state * state, 1, keepdims=True)
 
     took(es_v.at[pl.ds(0, NM - 1)], rsem.at[0])
     embed = es_v[0].astype(F32)
     for q in range(1, NM):
         embed = embed + es_v[q].astype(F32)
     scaled_e = (embed * gains[1:2]).astype(BF)
-    both = jnp.concatenate([scaled_h, scaled_e], 1)
-    squares = jnp.sum(state * state + embed * embed, 1, keepdims=True)
+    squares = squares_h + jnp.sum(embed * embed, 1, keepdims=True)
     squares = jnp.broadcast_to(squares, (ROWS, 128)).astype(BF)
-    low1 = mm(both, ad_v[...]).astype(BF)
-    for part in range(3):
-        proj = mm(both, wq_v[part]) + mm(low1, aup_v[part])
+
+    def project(part, dst, at):
+        proj = (ph_v[part] + mm(scaled_e, wq_v[part, pl.ds(FP, FP), :])).astype(BF)
         for j in range(NJ):
-            s2_v[j, :, pl.ds(128 * part, 128)] = proj[:, 128 * j : 128 * j + 128].astype(BF)
+            dst[j, :, pl.ds(at, 128)] = proj[:, 128 * j : 128 * j + 128]
+
+    def block_of(ref):
+        return lambda i, j: ref.at[j, pl.ds(pl.multiple_of(i * RT, RT), RT)]
+
     for j in range(NJ):
-        s2_v[j, :, pl.ds(384, 128)] = squares
-
-    def block2(i, j):
-        return s2_v.at[j, pl.ds(pl.multiple_of(i * RT, RT), RT)]
-
-    scatter(block2, r2_v.at[me_s], 1)
+        s2_v[j, :, pl.ds(128, 128)] = squares
+    project(0, s2_v, 0)
+    scatter(block_of(s2_v), r2_v.at[me_s], 1)
+    project(1, s2k_v, 0)
+    project(2, s2k_v, 128)
+    scatter(block_of(s2k_v), r2k_v.at[me_s], 2)
+    my_cols = pl.ds(pl.multiple_of(my_j * 128, 128), 128)
 
     @pl.when(mine)
     def _():
         r2_v[me_s] = s2_v[my_j, my_rows, :]
+        r2k_v[me_s] = s2k_v[my_j, my_rows, :]
         took(r2_v.at[pl.ds(0, NS - 1)], rsem.at[1])
         total = r2_v[0].astype(F32)
         for s in range(1, NS):
             total = total + r2_v[s].astype(F32)
-        scale = 1.0 / jnp.sqrt(total[:, 384:] / (2 * MODEL_WIDTH) + EPS)
-        for part in range(3):
-            g_v[my_j, my_rows, pl.ds(128 * part, 128)] = (
-                total[:, 128 * part : 128 * part + 128] * scale
-            ).astype(BF)
-        gather(g_v.at[my_j, my_rows], 2)
-        took(r2_v.at[pl.ds(0, OWN - 1), :, pl.ds(0, 384)], rsem.at[2])
+        scale = 1.0 / jnp.sqrt(total[:, 128:] / (2 * MODEL_WIDTH) + EPS)
+        block = gq_v.at[my_rows, my_cols]
+        block[...] = (total[:, :128] * scale).astype(BF)
+        gather(block, 3)
+        took(r2k_v.at[pl.ds(0, NS - 1)], rsem.at[2])
+        total = r2k_v[0].astype(F32)
+        for s in range(1, NS):
+            total = total + r2k_v[s].astype(F32)
+        scale = jnp.concatenate([scale, scale], 1)
+        g_v[my_j, my_rows, :] = (total * scale).astype(BF)
+        gather(g_v.at[my_j, my_rows], 4)
+        took(r2_v.at[pl.ds(0, OWN - 1), :, pl.ds(0, 128)], rsem.at[3])
 
     @pl.when(jnp.logical_not(mine))
     def _():
-        took(r2_v.at[pl.ds(0, OWN), :, pl.ds(0, 384)], rsem.at[2])
+        took(r2_v.at[pl.ds(0, OWN), :, pl.ds(0, 128)], rsem.at[3])
 
     lane = lax.broadcasted_iota(jnp.int32, (RT, 128), 1)
     for i in range(NI):
         rows = pl.ds(RT * i, RT)
         for c in range(NJ):
-            q = g_v[c, rows, pl.ds(0, 128)].astype(F32)
+            q = gq_v[rows, pl.ds(128 * c, 128)].astype(F32)
             first, last = (128 * c) // HEAD_DIM, (128 * c + 127) // HEAD_DIM
             for h in range(HEADS):
                 if first == last == h:
@@ -345,10 +382,15 @@
             s4_v[c, rows, pl.ds(0, 128)] = here.astype(BF)
             s4_v[c, rows, pl.ds(128, 128)] = stats
 
-    def block4(i, j):
-        return s4_v.at[j, pl.ds(pl.multiple_of(i * RT, RT), RT)]
-
-    scatter(block4, r4_v.at[me_s], 3)
+    scatter(block_of(s4_v), r4_v.at[me_s], 5)
+
+    @pl.when(mine)
+    def _():
+        took(r2_v.at[pl.ds(0, OWN - 1)], rsem.at[4])
+
+    @pl.when(jnp.logical_not(mine))
+    def _():
+        took(r2_v.at[pl.ds(0, OWN)], rsem.at[4])
 
     @pl.when(mine)
     def _():
@@ -356,9 +398,9 @@
         lane_head = head_of(lane + 128 * my_j)
         head_a = head_of(128 * my_j)
         head_b = head_of(128 * my_j + 127)
-        q = jnp.concatenate([g_v[c, my_rows, pl.ds(0, 128)] for c in range(NJ)], 1).astype(F32)
-        k = jnp.concatenate([g_v[c, my_rows, pl.ds(128, 128)] for c in range(NJ)], 1)
-        v = g_v[my_j, my_rows, pl.ds(256, 128)]
+        q = gq_v[my_rows, :].astype(F32)
+        k = jnp.concatenate([g_v[c, my_rows, pl.ds(0, 128)] for c in range(NJ)], 1)
+        v = g_v[my_j, my_rows, pl.ds(128, 128)]
         col_head = head_of(lax.broadcasted_iota(jnp.int32, (RT, CW), 1))
         r_at = lax.broadcasted_iota(jnp.int32, (RT, RT), 0)
         c_at = lax.broadcasted_iota(jnp.int32, (RT, RT), 1)
@@ -383,7 +425,7 @@
             .astype(F32)
             .astype(BF)
         )
-        took(r4_v.at[pl.ds(0, NS - 1)], rsem.at[3])
+        took(r4_v.at[pl.ds(0, NS - 1)], rsem.at[5])
         stats = r4_v[:, :, pl.ds(128, 128)].reshape(NS * RT, 128)
         lse = mm(stats, expand).reshape(NS, RT, 128)
         peak = jnp.maximum(jnp.max(lse, 0), new_lse)
@@ -391,18 +433,14 @@
         new_weight = jnp.exp(new_lse - peak)
         total = jnp.sum(weight, 0) + new_weight
         numer = jnp.sum(weight * r4_v[:, :, pl.ds(0, 128)].astype(F32), 0) + new_weight * new_out
-        block = a_v.at[my_rows, pl.ds(pl.multiple_of(my_j * 128, 128), 128)]
+        block = a_v.at[my_rows, my_cols]
         block[...] = (numer / total).astype(BF)
-        gather(block, 4)
+        gather(block, 6)
 
     for b in range(REQ):
         for c in range(NJ):
-            key_v[b, :, pl.ds(128 * c, 128)] = g_v[c, pl.ds(TOK * b, TOK), pl.ds(128, 128)]
-            val_v[b, :, pl.ds(128 * c, 128)] = g_v[c, pl.ds(TOK * b, TOK), pl.ds(256, 128)]
-    o_key = pltpu.make_async_copy(key_v, key_out, lsem.at[len(local)])
-    o_val = pltpu.make_async_copy(val_v, val_out, lsem.at[len(local) + 1])
-    o_key.start()
-    o_val.start()
+            key_v[b, :, pl.ds(128 * c, 128)] = g_v[c, pl.ds(TOK * b, TOK), pl.ds(0, 128)]
+            val_v[b, :, pl.ds(128 * c, 128)] = g_v[c, pl.ds(TOK * b, TOK), pl.ds(128, 128)]
     c_fup.wait()
 
     def split(k, carry):
@@ -413,65 +451,86 @@
         return carry
 
     lax.fori_loop(0, 8, split, 0)
-    c_wo.wait()
-
-    @pl.when(mine)
-    def _():
-        took(r4_v.at[pl.ds(0, OWN - 1), :, pl.ds(0, 128)], rsem.at[4])
-
-    @pl.when(jnp.logical_not(mine))
-    def _():
-        took(r4_v.at[pl.ds(0, OWN), :, pl.ds(0, 128)], rsem.at[4])
-
-    my_eight = pl.ds(pl.multiple_of(me_m * 8, 8), 8)
-
-    def sum_mp(part_v, slot_v, phase):
-        def fn(p):
-            send(
-                part_v.at[pl.ds(pl.multiple_of(p * 8, 8), 8)], slot_v.at[me_m], phase, "mp", p
-            )
-
-        loop(NM, me_m, fn)
-        slot_v[me_m] = part_v[my_eight, :]
-        took(slot_v.at[pl.ds(0, NM - 1)], rsem.at[phase])
-        total = slot_v[0]
-        for q in range(1, NM):
-            total = total + slot_v[q]
-        return total
-
-    hp_v[...] = mm_nt(a_v[...], wo_v[...])
-    mixed = sum_mp(hp_v, hr_v, 5)
-    mid_v[my_eight, :] = mixed + h_v[my_eight, :]
-    loop(NM, me_m, lambda p: send(mid_v.at[my_eight], mid_v.at[my_eight], 6, "mp", p))
     c_fg.wait()
     c_fd.wait()
     c_gate.wait()
     c_upm.wait()
+    for part, w_v in enumerate((gate_v, upm_v)):
+        w_v[...] = (w_v[...].astype(F32) + mm(fd_v[...], fu_v[part])).astype(BF)
+    c_wo.wait()
+
+    @pl.when(mine)
+    def _():
+        took(r4_v.at[pl.ds(0, OWN - 1), :, pl.ds(0, 128)], rsem.at[6])
+
+    @pl.when(jnp.logical_not(mine))
+    def _():
+        took(r4_v.at[pl.ds(0, OWN), :, pl.ds(0, 128)], rsem.at[6])
+
+    def sum_mp(part, slot_v, phase, meanwhile=lambda: None):
+        slot_v[me_m] = part.astype(BF)
+        each_mp(lambda p: send(slot_v.at[me_m], slot_v.at[me_m], phase, "mp", p))
+        meanwhile()
+        took(slot_v.at[pl.ds(0, NM - 1)], rsem.at[phase])
+        total = slot_v[0].astype(F32)
+        for q in range(1, NM):
+            total = total + slot_v[q].astype(F32)
+        return total
+
+    mixed = sum_mp(mm_nt(a_v[...], wo_v[...]), hr_v, 7)
+    mid_v[...] = mixed + h_v[...]
     fgain = jnp.concatenate([fgain_v[...].astype(F32), jnp.zeros((1, pad), F32)], 1)
-    took(hr_v.at[pl.ds(0, NM - 1)], rsem.at[6])
 
     mid = mid_v[...]
     scaled_m = (mid * fgain).astype(BF)
-    squares = jnp.broadcast_to(jnp.sum(mid * mid, 1, keepdims=True), (ROWS, 128)).astype(BF)
-    low2 = mm(scaled_m, fd_v[...]).astype(BF)
-    for part, w_v in enumerate((gate_v, upm_v)):
-        proj = mm(scaled_m, w_v[...]) + mm(low2, fu_v[part])
-        for j in range(NJ):
-            s7_v[j, :, pl.ds(256 * part, 256)] = proj[:, 256 * j : 256 * j + 256].astype(BF)
-    for j in range(NJ):
-        s7_v[j, :, pl.ds(512, 128)] = squares
+    squares = jnp.broadcast_to(jnp.sum(mid * mid, 1, keepdims=True), (ROWS, 128))
+
+    def partial(j):
+        at = pl.ds(pl.multiple_of(j * 256, 256), 256)
+        return jnp.concatenate(
+            [mm(scaled_m, gate_v[:, at]), mm(scaled_m, upm_v[:, at]), squares], 1
+        )
+
+    sibling = me_s + 1 - 2 * core
+    for k in range(4):
+        x7_v[0, k] = partial(3 * (1 - core) + k).astype(BF)
+    send(x7_v.at[0], x7_v.at[1], 11, "seq", sibling)
+    for k in range(4):
+        p7_v[k] = partial(3 * core + k)
+    took(x7_v.at[1], rsem.at[11])
+    for k in range(4):
+        s7_v[k] = (p7_v[k] + x7_v[1, k].astype(F32)).astype(BF)
+
+    def sent_here(i, j):
+        upper = jnp.where(i >= NI // 2, 1, 0)
+        return jnp.where(j < 3, 0, jnp.where(j > 3, 1, upper)) == core
 
     def block7(i, j):
-        return s7_v.at[j, pl.ds(pl.multiple_of(i * RT, RT), RT)]
-
-    scatter(block7, r7_v.at[me_s], 7)
+        return s7_v.at[j - 3 * core, pl.ds(pl.multiple_of(i * RT, RT), RT)]
+
+    def send7(p):
+        i, j = lax.div(p, NJ), lax.rem(p, NJ)
+
+        @pl.when((p < OWN) & sent_here(i, j))
+        def _():
+            send(block7(i, j), r7_v.at[lax.div(me_s, 2)], 8, "seq", p)
+
+    each_seq(send7)
+    own_block = mine & sent_here(my_i, my_j)
 
     @pl.when(mine)
     def _():
-        r7_v[me_s] = s7_v[my_j, my_rows, :]
-        took(r7_v.at[pl.ds(0, NS - 1)], rsem.at[7])
+        @pl.when(own_block)
+        def _():
+            r7_v[lax.div(me_s, 2)] = s7_v[my_j - 3 * core, my_rows, :]
+            took(r7_v.at[pl.ds(0, NS // 2 - 1)], rsem.at[8])
+
+        @pl.when(jnp.logical_not(own_block))
+        def _():
+            took(r7_v.at[pl.ds(0, NS // 2)], rsem.at[8])
+
         total = r7_v[0].astype(F32)
-        for s in range(1, NS):
+        for s in range(1, NS // 2):
             total = total + r7_v[s].astype(F32)
         scale = 1.0 / jnp.sqrt(total[:, 512:] / MODEL_WIDTH + EPS)
         scale = jnp.concatenate([scale, scale], 1)
@@ -479,48 +538,47 @@
         up = total[:, 256:512] * scale
         block = a2_v.at[my_rows, pl.ds(pl.multiple_of(my_j * 256, 256), 256)]
         block[...] = (jax.nn.gelu(gate, approximate=True) * up).astype(BF)
-        gather(block, 8)
-        took(r4_v.at[pl.ds(0, OWN - 1)], rsem.at[8])
+        gather(block, 9)
+        took(r4_v.at[pl.ds(0, OWN - 1)], rsem.at[9])
 
     @pl.when(jnp.logical_not(mine))
     def _():
-        took(r4_v.at[pl.ds(0, OWN)], rsem.at[8])
+        took(r4_v.at[pl.ds(0, OWN)], rsem.at[9])
 
     c_dn.wait()
-    dp_v[...] = mm_nt(a2_v[...], dn_v[...])
-    down = sum_mp(dp_v, dr_v, 9)
-    fin_v[my_eight, :] = down + mid_v[my_eight, :]
-    loop(NM, me_m, lambda p: send(fin_v.at[my_eight], fin_v.at[my_eight], 10, "mp", p))
-    took(dr_v.at[pl.ds(0, NM - 1)], rsem.at[10])
+    down = sum_mp(mm_nt(a2_v[...], dn_v[...]), dr_v, 10)
+    updated = (down + mid_v[...]).astype(BF)
     for b in range(REQ):
-        upd_v[b] = fin_v[pl.ds(TOK * b, TOK), pl.ds(0, F)].astype(BF)
-    o_upd = pltpu.make_async_copy(upd_v, upd_out, lsem.at[len(local) + 2])
-    o_upd.start()
+        upd_v[b] = updated[TOK * b : TOK * b + TOK, :F]
 
     took(es_v.at[pl.ds(0, NM - 1)], ssem.at[0])
-    took(hr_v.at[pl.ds(0, NM - 1)], ssem.at[5])
-    took(hr_v.at[pl.ds(0, NM - 1)], ssem.at[6])
-    took(dr_v.at[pl.ds(0, NM - 1)], ssem.at[9])
+    took(hr_v.at[pl.ds(0, NM - 1)], ssem.at[7])
     took(dr_v.at[pl.ds(0, NM - 1)], ssem.at[10])
+    took(x7_v.at[1], ssem.at[11])
+
+    @pl.when(own_block)
+    def _():
+        took(r7_v.at[pl.ds(0, OWN // 2 - 1)], ssem.at[8])
+
+    @pl.when(jnp.logical_not(own_block))
+    def _():
+        took(r7_v.at[pl.ds(0, OWN // 2)], ssem.at[8])
 
     @pl.when(mine)
     def _():
         took(r2_v.at[pl.ds(0, OWN - 1)], ssem.at[1])
-        took(r2_v.at[pl.ds(0, NS - 1), :, pl.ds(0, 384)], ssem.at[2])
-        took(r4_v.at[pl.ds(0, OWN - 1)], ssem.at[3])
-        took(r4_v.at[pl.ds(0, NS - 1), :, pl.ds(0, 128)], ssem.at[4])
-        took(r7_v.at[pl.ds(0, OWN - 1)], ssem.at[7])
-        took(r4_v.at[pl.ds(0, NS - 1)], ssem.at[8])
+        took(r2k_v.at[pl.ds(0, OWN - 1)], ssem.at[2])
+        took(r2_v.at[pl.ds(0, NS - 1), :, pl.ds(0, 128)], ssem.at[3])
+        took(r2_v.at[pl.ds(0, NS - 1)], ssem.at[4])
+        took(r4_v.at[pl.ds(0, OWN - 1)], ssem.at[5])
+        took(r4_v.at[pl.ds(0, NS - 1), :, pl.ds(0, 128)], ssem.at[6])
+        took(r4_v.at[pl.ds(0, NS - 1)], ssem.at[9])
 
     @pl.when(jnp.logical_not(mine))
     def _():
         took(r2_v.at[pl.ds(0, OWN)], ssem.at[1])
-        took(r4_v.at[pl.ds(0, OWN)], ssem.at[3])
-        took(r7_v.at[pl.ds(0, OWN)], ssem.at[7])
-
-    o_key.wait()
-    o_val.wait()
-    o_upd.wait()
+        took(r2k_v.at[pl.ds(0, OWN)], ssem.at[2])
+        took(r4_v.at[pl.ds(0, OWN)], ssem.at[5])
 
 
 def per_device(
@@ -543,17 +601,14 @@
     down_matrix,
 ):
     hbm = pl.BlockSpec(memory_space=pl.ANY)
+    inner = pl.BlockSpec(memory_space=pltpu.VMEM)
     vm = pltpu.VMEM
     return pl.pallas_call(
         kernel,
         name="block",
-        out_shape=(
-            jax.ShapeDtypeStruct((REQ, TOK, F), BF),
-            jax.ShapeDtypeStruct((REQ, TOK, CW), BF),
-            jax.ShapeDtypeStruct((REQ, TOK, CW), BF),
-        ),
+        out_shape=(vm((REQ, TOK, F), BF), vm((REQ, TOK, CW), BF), vm((REQ, TOK, CW), BF)),
         in_specs=[hbm] * 17,
-        out_specs=(hbm, hbm, hbm),
+        out_specs=(inner, inner, inner),
         scratch_shapes=[
             vm((TOK, REQ), jnp.int32),
             pltpu.SMEM((REQ,), jnp.int32),
@@ -574,29 +629,29 @@
             vm((2, 128, UW), BF),
             vm((FP, UW), BF),
             vm((ROWS, FP), F32),
+            vm((3, ROWS, CW), F32),
             vm((NM, ROWS, FP), BF),
-            vm((NJ, ROWS, 512), BF),
-            vm((NS, RT, 512), BF),
-            vm((NJ, ROWS, 384), BF),
+            vm((NJ, ROWS, 256), BF),
+            vm((NS, RT, 256), BF),
+            vm((NJ, ROWS, 256), BF),
+            vm((NS, RT, 256), BF),
+            vm((ROWS, CW), BF),
+            vm((NJ, ROWS, 256), BF),
             vm((NI, HEADS * RT, CW), BF),
             vm((NJ, ROWS, 256), BF),
             vm((NS, RT, 256), BF),
             vm((ROWS, CW), BF),
+            vm((NM, ROWS, FP), BF),
             vm((ROWS, FP), F32),
-            vm((NM, 8, FP), F32),
-            vm((ROWS, FP), F32),
-            vm((NJ, ROWS, 640), BF),
-            vm((NS, RT, 640), BF),
+            vm((2, 4, ROWS, 640), BF),
+            vm((4, ROWS, 640), F32),
+            vm((4, ROWS, 640), BF),
+            vm((NS // 2, RT, 640), BF),
             vm((ROWS, UW), BF),
-            vm((ROWS, FP), F32),
-            vm((NM, 8, FP), F32),
-            vm((ROWS, FP), F32),
-            vm((REQ, TOK, F), BF),
-            vm((REQ, TOK, CW), BF),
-            vm((REQ, TOK, CW), BF),
+            vm((NM, ROWS, FP), BF),
             pltpu.SemaphoreType.DMA((24,)),
-            pltpu.SemaphoreType.DMA((11,)),
-            pltpu.SemaphoreType.DMA((11,)),
+            pltpu.SemaphoreType.DMA((12,)),
+            pltpu.SemaphoreType.DMA((12,)),
         ],
         compiler_params=pltpu.CompilerParams(
             collective_id=0, has_side_effects=True, vmem_limit_bytes=56 * 1024 * 1024

time: 90.2 us -> 68.6 us (0.76)
  Pallas kernels: 83.9 us -> 65.3 us
  local copies, waits for them, and re-layouts: 4.5 us -> 1.9 us
    pallas_call x1, Pallas kernels: 83.9 us -> 65.3 us  [per_device(): pl.pallas_call(kernel, name='block', out_shape=(vm((REQ, TOK, F), BF), vm...]
    unnamed x3, local copies, waits for them, and re-layouts: 4.5 us -> 1.9 us
where the time goes in v2:
time: 68.6 us; the launch traced here: 67.9 us
  Pallas kernels  65.3 us (95%)
  local copies, waits for them, and re-layouts  1.9 us (3%)
    pallas_call x1, Pallas kernels, per_device(): pl.pallas_call(kernel, name='block', out_shape=(vm((REQ, TOK, F), BF), vm...  65.3 us
    unnamed x3, local copies, waits for them, and re-layouts  1.9 us

profile of v2, /device:TPU:32, one launch (start us, length us, event | category | flops | bytes accessed | tf_op | source)
XLA Modules:
  0.0 67.9 jit_solution(16552175492542368343)
XLA Ops:
  0.6 65.3 %block.1 = (bf16[16,4,112]{2,1,0:T(4,128)(2,1)S(1)}, bf16[16,4,896]{2,1,0:T(4,128)(2,1)S(1)}, bf16[16,4,896]{2,1,0:T(4,128)(2,1)S(1)}) custom-call(s32[4,16]{1,0:T(4,128)} %bitcast.12, s32[16]{0:T(128)} %len_hbm.1, bf16[16,4,112]{2,1,0:T(4,128)(2,1)} %hid_hbm.1, bf16[112,4000]{1,0:T(8,128)(2,1)} %bitcast.8, bf16[2,112]{1,0:T(2,128)(2,1)} %gain_hbm.1, ...), custom_call_target="tpu_custom_call" | custom-call | tf_op jit(solution)/shard_map/block/pallas_call | solution.py:606
  66.0 0.6 copy.23
  66.6 0.6 copy.24
  67.2 0.6 copy.25

commit v3 on v2

--- a/solution.py
+++ b/solution.py
@@ -34,7 +34,7 @@
 
 SEQ_ORDER = sorted(
     ((dx, dy, dc) for dx in range(4) for dy in range(4) for dc in range(2) if dx or dy or dc),
-    key=lambda offset: -hops(offset),
+    key=lambda offset: (-hops(offset), offset[2]),
 )
 MP_ORDER = (4, 3, 5, 2, 6, 1, 7)
 
@@ -115,6 +115,7 @@
     s4_v,
     r4_v,
     a_v,
+    scale_v,
     hr_v,
     mid_v,
     x7_v,
@@ -174,21 +175,6 @@
     c_emb = fetch(emb_hbm, emb_v)
     c_hid = fetch(hid_hbm, hid_v)
     c_gain = fetch(gain_hbm, gain_v)
-    c_ad0 = fetch(adown_hbm.at[0], ad_v.at[pl.ds(0, F)])
-    c_ad1 = fetch(adown_hbm.at[1], ad_v.at[pl.ds(FP, F)])
-    c_wq0 = fetch(wqkv_hbm.at[0], wq_v.at[:, pl.ds(0, F)])
-    c_wq1 = fetch(wqkv_hbm.at[1], wq_v.at[:, pl.ds(FP, F)])
-    c_aup = fetch(aup_hbm, aup_v)
-    c_len = fetch(len_hbm, len_s)
-    c_kc = fetch(kc_hbm, kc_v)
-    c_vc = fetch(vc_hbm, vc_v)
-    c_wo = fetch(wout_hbm, wo_v.at[pl.ds(0, F)])
-    c_fg = fetch(fgain_hbm, fgain_v)
-    c_fup = fetch(fup_hbm, fup_v)
-    c_fd = fetch(fdown_hbm, fd_v.at[pl.ds(0, F)])
-    c_gate = fetch(gate_hbm, gate_v.at[pl.ds(0, F)])
-    c_upm = fetch(upm_hbm, upm_v.at[pl.ds(0, F)])
-    c_dn = fetch(down_hbm, dn_v.at[pl.ds(0, F)])
 
     pad = FP - F
     wq_v[:, pl.ds(F, pad), :] = jnp.zeros((3, pad, CW), BF)
@@ -244,6 +230,11 @@
         (lax.broadcasted_iota(jnp.int32, (VR, ROWS), 0) == id_row).astype(F32).astype(BF)
     )
     c_emb.wait()
+    c_ad0 = fetch(adown_hbm.at[0], ad_v.at[pl.ds(0, F)])
+    c_ad1 = fetch(adown_hbm.at[1], ad_v.at[pl.ds(FP, F)])
+    c_wq0 = fetch(wqkv_hbm.at[0], wq_v.at[:, pl.ds(0, F)])
+    c_wq1 = fetch(wqkv_hbm.at[1], wq_v.at[:, pl.ds(FP, F)])
+    c_aup = fetch(aup_hbm, aup_v)
     found = mm(emb_v[...], selector)
     found = jnp.concatenate([found, jnp.zeros((pad, ROWS), F32)], 0)
     es_v[me_m] = found.T.astype(BF)
@@ -252,6 +243,16 @@
 
     each_mp(lambda p: send(es_v.at[me_m], es_v.at[me_m], 0, "mp", p))
 
+    c_len = fetch(len_hbm, len_s)
+    c_kc = fetch(kc_hbm, kc_v)
+    c_vc = fetch(vc_hbm, vc_v)
+    c_wo = fetch(wout_hbm, wo_v.at[pl.ds(0, F)])
+    c_fg = fetch(fgain_hbm, fgain_v)
+    c_fup = fetch(fup_hbm, fup_v)
+    c_fd = fetch(fdown_hbm, fd_v.at[pl.ds(0, F)])
+    c_gate = fetch(gate_hbm, gate_v.at[pl.ds(0, F)])
+    c_upm = fetch(upm_hbm, upm_v.at[pl.ds(0, F)])
+    c_dn = fetch(down_hbm, dn_v.at[pl.ds(0, F)])
     c_hid.wait()
     c_gain.wait()
     for b in range(REQ):
@@ -280,7 +281,14 @@
         embed = embed + es_v[q].astype(F32)
     scaled_e = (embed * gains[1:2]).astype(BF)
     squares = squares_h + jnp.sum(embed * embed, 1, keepdims=True)
-    squares = jnp.broadcast_to(squares, (ROWS, 128)).astype(BF)
+    on_lane = lax.broadcasted_iota(jnp.int32, (ROWS, 128), 0) == lax.broadcasted_iota(
+        jnp.int32, (ROWS, 128), 1
+    )
+    squares = jnp.sum(jnp.where(on_lane, squares, 0.0), 0, keepdims=True)
+    squares = jnp.broadcast_to(squares, (8, 128))
+    lead = squares.astype(BF).astype(F32)
+    upper_half = lax.broadcasted_iota(jnp.int32, (8, 128), 0) < 4
+    squares = jnp.where(upper_half, lead, squares - lead).astype(BF)
 
     def project(part, dst, at):
         proj = (ph_v[part] + mm(scaled_e, wq_v[part, pl.ds(FP, FP), :])).astype(BF)
@@ -290,10 +298,22 @@
     def block_of(ref):
         return lambda i, j: ref.at[j, pl.ds(pl.multiple_of(i * RT, RT), RT)]
 
-    for j in range(NJ):
-        s2_v[j, :, pl.ds(128, 128)] = squares
-    project(0, s2_v, 0)
-    scatter(block_of(s2_v), r2_v.at[me_s], 1)
+    proj = (ph_v[0] + mm(scaled_e, wq_v[0, pl.ds(FP, FP), :])).astype(BF)
+    for i in range(NI):
+        for j in range(NJ):
+            s2_v[i * NJ + j, pl.ds(0, RT), :] = proj[RT * i : RT * i + RT, 128 * j : 128 * j + 128]
+            s2_v[i * NJ + j, pl.ds(RT, 8), :] = squares
+    scatter(lambda i, j: s2_v.at[i * NJ + j], r2_v.at[me_s], 1)
+    c_fup.wait()
+
+    def split(k, carry):
+        at = pl.ds(pl.multiple_of(k * 16, 16), 16)
+        two = fup_v[at].astype(F32)
+        fu_v[0, at, :] = two[:, 0, :].astype(BF)
+        fu_v[1, at, :] = two[:, 1, :].astype(BF)
+        return carry
+
+    lax.fori_loop(0, 8, split, 0)
     project(1, s2k_v, 0)
     project(2, s2k_v, 128)
     scatter(block_of(s2k_v), r2k_v.at[me_s], 2)
@@ -301,28 +321,45 @@
 
     @pl.when(mine)
     def _():
-        r2_v[me_s] = s2_v[my_j, my_rows, :]
+        r2_v[me_s] = s2_v[me_s]
         r2k_v[me_s] = s2k_v[my_j, my_rows, :]
         took(r2_v.at[pl.ds(0, NS - 1)], rsem.at[1])
         total = r2_v[0].astype(F32)
         for s in range(1, NS):
             total = total + r2_v[s].astype(F32)
-        scale = 1.0 / jnp.sqrt(total[:, 128:] / (2 * MODEL_WIDTH) + EPS)
+        sums = jnp.broadcast_to(total[RT : RT + 1] + total[RT + 4 : RT + 5], (RT, 128))
+        row_at = lax.broadcasted_iota(jnp.int32, (RT, 128), 0) + my_i * RT
+        here = lax.broadcasted_iota(jnp.int32, (RT, 128), 1) == row_at
+        sums = jnp.sum(jnp.where(here, sums, 0.0), 1, keepdims=True)
+        scale = jnp.broadcast_to(
+            1.0 / jnp.sqrt(sums / (2 * MODEL_WIDTH) + EPS), (RT, 128)
+        )
         block = gq_v.at[my_rows, my_cols]
-        block[...] = (total[:, :128] * scale).astype(BF)
+        block[...] = (total[:RT] * scale).astype(BF)
+        scale_v[...] = scale
         gather(block, 3)
+
+    c_fg.wait()
+    c_fd.wait()
+    c_gate.wait()
+    c_upm.wait()
+    for part, w_v in enumerate((gate_v, upm_v)):
+        w_v[...] = (w_v[...].astype(F32) + mm(fd_v[...], fu_v[part])).astype(BF)
+
+    @pl.when(mine)
+    def _():
         took(r2k_v.at[pl.ds(0, NS - 1)], rsem.at[2])
         total = r2k_v[0].astype(F32)
         for s in range(1, NS):
             total = total + r2k_v[s].astype(F32)
-        scale = jnp.concatenate([scale, scale], 1)
+        scale = jnp.concatenate([scale_v[...], scale_v[...]], 1)
         g_v[my_j, my_rows, :] = (total * scale).astype(BF)
         gather(g_v.at[my_j, my_rows], 4)
-        took(r2_v.at[pl.ds(0, OWN - 1), :, pl.ds(0, 128)], rsem.at[3])
+        took(r2k_v.at[pl.ds(0, OWN - 1), :, pl.ds(0, 128)], rsem.at[3])
 
     @pl.when(jnp.logical_not(mine))
     def _():
-        took(r2_v.at[pl.ds(0, OWN), :, pl.ds(0, 128)], rsem.at[3])
+        took(r2k_v.at[pl.ds(0, OWN), :, pl.ds(0, 128)], rsem.at[3])
 
     lane = lax.broadcasted_iota(jnp.int32, (RT, 128), 1)
     for i in range(NI):
@@ -345,24 +382,34 @@
     c_vc.wait()
     place = me_s * POS + lax.broadcasted_iota(jnp.int32, (HEADS * RT, POS), 1)
     group = (lax.broadcasted_iota(jnp.int32, (HEADS * RT, POS), 0) % RT) // TOK
+    per = RT // TOK
+    scores = []
     for i in range(NI):
         score = jnp.full((HEADS * RT, POS), DEAD, F32)
-        for k in range(RT // TOK):
-            b = (RT // TOK) * i + k
+        for k in range(per):
+            b = per * i + k
             one = mm_nt(qm_v[i], kc_v[b]) * inv_scale
             score = jnp.where((group == k) & (place < len_s[b]), one, score)
-        peak = jnp.max(score, 1, keepdims=True)
-        weight = jnp.where(score > 0.5 * DEAD, jnp.exp(score - peak), 0.0)
-        total = jnp.sum(weight, 1, keepdims=True)
+        scores.append(score)
+    peaks = [jnp.max(score, 1, keepdims=True) for score in scores]
+    weights = [
+        jnp.where(score > 0.5 * DEAD, jnp.exp(score - peak), 0.0)
+        for score, peak in zip(scores, peaks)
+    ]
+    totals = [jnp.sum(weight, 1, keepdims=True) for weight in weights]
+    numers = []
+    for i in range(NI):
         spread_w = jnp.concatenate(
-            [jnp.where(group == k, weight, 0.0).astype(BF) for k in range(RT // TOK)], 1
+            [jnp.where(group == k, weights[i], 0.0).astype(BF) for k in range(per)], 1
         )
-        values = vc_v[pl.ds((RT // TOK) * i, RT // TOK)].reshape((RT // TOK) * POS, CW)
-        numer = mm(spread_w, values)
-        live = total > 0.0
-        safe = jnp.where(live, total, 1.0)
-        lse = jnp.where(live, peak + jnp.log(safe), DEAD)
-        inverse = 1.0 / safe
+        values = vc_v[pl.ds(per * i, per)].reshape(per * POS, CW)
+        numers.append(mm(spread_w, values))
+    inverses = []
+    for i in range(NI):
+        live = totals[i] > 0.0
+        safe = jnp.where(live, totals[i], 1.0)
+        lse = jnp.where(live, peaks[i] + jnp.log(safe), DEAD)
+        inverses.append(1.0 / safe)
         stats = jnp.zeros((RT, 128), F32)
         for h in range(HEADS):
             rest = jnp.broadcast_to(lse[RT * h : RT * h + RT], (RT, 128))
@@ -371,7 +418,10 @@
                 stats = jnp.where(lane == 3 * h + piece, lead, stats)
                 rest = rest - lead
         stats = stats.astype(BF)
-        rows = pl.ds(RT * i, RT)
+        for c in range(NJ):
+            s4_v[c, pl.ds(RT * i, RT), pl.ds(128, 128)] = stats
+    for i in range(NI):
+        numer, inverse = numers[i], inverses[i]
         for c in range(NJ):
             first, last = (128 * c) // HEAD_DIM, (128 * c + 127) // HEAD_DIM
             cols = slice(128 * c, 128 * c + 128)
@@ -379,18 +429,22 @@
             if last != first:
                 there = numer[RT * last : RT * last + RT, cols] * inverse[RT * last : RT * last + RT]
                 here = jnp.where(head_of(lane + 128 * c) == first, here, there)
-            s4_v[c, rows, pl.ds(0, 128)] = here.astype(BF)
-            s4_v[c, rows, pl.ds(128, 128)] = stats
-
-    scatter(block_of(s4_v), r4_v.at[me_s], 5)
+            s4_v[c, pl.ds(RT * i, RT), pl.ds(0, 128)] = here.astype(BF)
+        for j in range(NJ):
+            p = NJ * i + j
+
+            @pl.when(me_s != p)
+            def _(i=i, j=j, p=p):
+                send(s4_v.at[j, pl.ds(RT * i, RT)], r4_v.at[me_s], 5, "seq", p)
+
 
     @pl.when(mine)
     def _():
-        took(r2_v.at[pl.ds(0, OWN - 1)], rsem.at[4])
+        took(r2k_v.at[pl.ds(0, OWN - 1)], rsem.at[4])
 
     @pl.when(jnp.logical_not(mine))
     def _():
-        took(r2_v.at[pl.ds(0, OWN)], rsem.at[4])
+        took(r2k_v.at[pl.ds(0, OWN)], rsem.at[4])
 
     @pl.when(mine)
     def _():
@@ -441,22 +495,6 @@
         for c in range(NJ):
             key_v[b, :, pl.ds(128 * c, 128)] = g_v[c, pl.ds(TOK * b, TOK), pl.ds(0, 128)]
             val_v[b, :, pl.ds(128 * c, 128)] = g_v[c, pl.ds(TOK * b, TOK), pl.ds(128, 128)]
-    c_fup.wait()
-
-    def split(k, carry):
-        at = pl.ds(pl.multiple_of(k * 16, 16), 16)
-        two = fup_v[at].astype(F32)
-        fu_v[0, at, :] = two[:, 0, :].astype(BF)
-        fu_v[1, at, :] = two[:, 1, :].astype(BF)
-        return carry
-
-    lax.fori_loop(0, 8, split, 0)
-    c_fg.wait()
-    c_fd.wait()
-    c_gate.wait()
-    c_upm.wait()
-    for part, w_v in enumerate((gate_v, upm_v)):
-        w_v[...] = (w_v[...].astype(F32) + mm(fd_v[...], fu_v[part])).astype(BF)
     c_wo.wait()
 
     @pl.when(mine)
@@ -568,8 +606,8 @@
     def _():
         took(r2_v.at[pl.ds(0, OWN - 1)], ssem.at[1])
         took(r2k_v.at[pl.ds(0, OWN - 1)], ssem.at[2])
-        took(r2_v.at[pl.ds(0, NS - 1), :, pl.ds(0, 128)], ssem.at[3])
-        took(r2_v.at[pl.ds(0, NS - 1)], ssem.at[4])
+        took(r2k_v.at[pl.ds(0, NS - 1), :, pl.ds(0, 128)], ssem.at[3])
+        took(r2k_v.at[pl.ds(0, NS - 1)], ssem.at[4])
         took(r4_v.at[pl.ds(0, OWN - 1)], ssem.at[5])
         took(r4_v.at[pl.ds(0, NS - 1), :, pl.ds(0, 128)], ssem.at[6])
         took(r4_v.at[pl.ds(0, NS - 1)], ssem.at[9])
@@ -579,6 +617,17 @@
         took(r2_v.at[pl.ds(0, OWN)], ssem.at[1])
         took(r2k_v.at[pl.ds(0, OWN)], ssem.at[2])
         took(r4_v.at[pl.ds(0, OWN)], ssem.at[5])
+
+
+def hand_on(a, b, c, a_out, b_out, c_out, sem):
+    copies = [
+        pltpu.make_async_copy(src, dst, sem.at[k])
+        for k, (src, dst) in enumerate(((a, a_out), (b, b_out), (c, c_out)))
+    ]
+    for copy in copies:
+        copy.start()
+    for copy in copies:
+        copy.wait()
 
 
 def per_device(
@@ -603,7 +652,7 @@
     hbm = pl.BlockSpec(memory_space=pl.ANY)
     inner = pl.BlockSpec(memory_space=pltpu.VMEM)
     vm = pltpu.VMEM
-    return pl.pallas_call(
+    results = pl.pallas_call(
         kernel,
         name="block",
         out_shape=(vm((REQ, TOK, F), BF), vm((REQ, TOK, CW), BF), vm((REQ, TOK, CW), BF)),
@@ -631,8 +680,8 @@
             vm((ROWS, FP), F32),
             vm((3, ROWS, CW), F32),
             vm((NM, ROWS, FP), BF),
-            vm((NJ, ROWS, 256), BF),
-            vm((NS, RT, 256), BF),
+            vm((OWN, RT + 8, 128), BF),
+            vm((NS, RT + 8, 128), BF),
             vm((NJ, ROWS, 256), BF),
             vm((NS, RT, 256), BF),
             vm((ROWS, CW), BF),
@@ -641,6 +690,7 @@
             vm((NJ, ROWS, 256), BF),
             vm((NS, RT, 256), BF),
             vm((ROWS, CW), BF),
+            vm((RT, 128), F32),
             vm((NM, ROWS, FP), BF),
             vm((ROWS, FP), F32),
             vm((2, 4, ROWS, 640), BF),
@@ -675,6 +725,15 @@
         feedforward_adapter_up,
         down_matrix.T,
     )
+    results = [pltpu.with_memory_space_constraint(r, pltpu.VMEM) for r in results]
+    return pl.pallas_call(
+        hand_on,
+        name="hand_on",
+        out_shape=tuple(jax.ShapeDtypeStruct(r.shape, BF) for r in results),
+        in_specs=[inner] * 3,
+        out_specs=(hbm, hbm, hbm),
+        scratch_shapes=[pltpu.SemaphoreType.DMA((3,))],
+    )(*results)
 
 
 def solution(mesh):

time: 68.6 us -> 65.9 us (0.961)
  local copies, waits for them, and re-layouts: 1.9 us -> 0 us
  Pallas kernels: 65.3 us -> 64.3 us
    unnamed x3 -> x0, local copies, waits for them, and re-layouts: 1.9 us -> none
    pallas_call x1, Pallas kernels: 65.3 us -> 63.6 us  [per_device(): pl.pallas_call(kernel, name='block', out_shape=(vm((REQ, TOK, F), BF), vm...]
    pallas_call x0 -> x1, Pallas kernels: none -> 0.72 us  [per_device(): pl.pallas_call(hand_on, name='hand_on', out_shape=tuple((jax.ShapeDtypeSt...]
where the time goes in v3:
time: 65.9 us; the launch traced here: 65 us
  Pallas kernels  64.3 us (98%)
    pallas_call x1, Pallas kernels, per_device(): pl.pallas_call(kernel, name='block', out_shape=(vm((REQ, TOK, F), BF), vm...  63.6 us

profile of v3, /device:TPU:32, one launch (start us, length us, event | category | flops | bytes accessed | tf_op | source)
XLA Modules:
  0.0 65.0 jit_solution(4639440265500614446)
XLA Ops:
  0.6 63.6 %block.1 = (bf16[16,4,112]{2,1,0:T(4,128)(2,1)S(1)}, bf16[16,4,896]{2,1,0:T(4,128)(2,1)S(1)}, bf16[16,4,896]{2,1,0:T(4,128)(2,1)S(1)}) custom-call(s32[4,16]{1,0:T(4,128)} %bitcast.12, s32[16]{0:T(128)} %len_hbm.1, bf16[16,4,112]{2,1,0:T(4,128)(2,1)} %hid_hbm.1, bf16[112,4000]{1,0:T(8,128)(2,1)} %bitcast.8, bf16[2,112]{1,0:T(2,128)(2,1)} %gain_hbm.1, ...), custom_call_target="tpu_custom_call" | custom-call | tf_op jit(solution)/shard_map/block/pallas_call | solution.py:655
  64.3 0.7 %hand_on.1 = (bf16[16,4,112]{2,1,0:T(4,128)(2,1)}, bf16[16,4,896]{2,1,0:T(4,128)(2,1)}, bf16[16,4,896]{2,1,0:T(4,128)(2,1)}) custom-call(bf16[16,4,112]{2,1,0:T(4,128)(2,1)S(1)} %get-tuple-element.6.a, bf16[16,4,896]{2,1,0:T(4,128)(2,1)S(1)} %get-tuple-element.7.b, bf16[16,4,896]{2,1,0:T(4,128)(2,1)S(1)} %get-tuple-element.8.c), custom_call_target="tpu_custom_call" | custom-call | tf_op jit(solution)/shard_map/hand_on/pallas_call | solution.py:729
